TPU v7x, 256 devices: a whole 4x4x8 slice. The times are simulated.
256 devices in a mesh: cell: 16 (over z_lo, x, core), gene: 16 (over y, z_hi).
Axes of the slice: x: 4, y: 4, z: 8 (z_hi: 4, z_lo: 2; z = z_hi * 2 + z_lo), core: 2. Of those that a mesh axis runs over, the one named last changes fastest.
Arguments:
- counts: int32 [16384, 8192], P('cell', 'gene'), may hold values from 0 to 4000, as said below
Outputs:
- gene_gram: float32 [8192, 8192], P('gene', 'cell')
Inputs may be any that keep to these rules, and one draw needn't show every extreme that they name: `counts`: every cell and every gene has a positive count somewhere.
All inputs are finite; a program needn't handle non-finite values.
Results may differ from a plain program's by a relative error of at most 0.00054.
Values may be sent and summed in bfloat16 or wider, within the bound.
A program may use at most 128 MiB of HBM per device.

v0:
```python
import jax
import jax.numpy as jnp
from jax import lax
from jax.sharding import PartitionSpec as P


def body(counts):
    cells_all = counts.shape[0] * lax.axis_size("cell")
    values = counts.astype(jnp.float32)
    row_part = jnp.sum(values, axis=1)
    column_part = jnp.sum(values, axis=0)
    depths = lax.psum(row_part, "gene")
    gene_totals = lax.psum(column_part, "cell")
    grand_total = lax.psum(jnp.sum(row_part), ("cell", "gene"))
    expected = depths[:, None] * gene_totals[None, :] / grand_total
    scaled = (values - expected) / jnp.sqrt(expected + expected * expected / 100.0)
    ceiling = jnp.sqrt(jnp.float32(cells_all))
    residuals = jnp.clip(scaled, -ceiling, ceiling).astype(jnp.bfloat16)
    gathered = lax.all_gather(residuals, "gene", axis=1, tiled=True)
    owned_block = lax.psum_scatter(
        lax.dot_general(
            gathered, residuals, (((0,), (0,)), ((), ())), preferred_element_type=jnp.float32
        ),
        "cell",
        scatter_dimension=0,
        tiled=True,
    ).T
    return owned_block / jnp.float32(cells_all)


def solution(mesh):
    return jax.shard_map(
        body,
        mesh=mesh,
        in_specs=(P("cell", "gene"),),
        out_specs=P("gene", "cell"),
        check_vma=False,
    )
```

profile of v0, /device:TPU:33, one launch (start us, length us, event | category | flops | bytes accessed | tf_op | source)
XLA Modules:
  0.0 486.3 jit_solution(18301592242679474501)
XLA Ops:
  6.5 0.0 copy-start
  6.5 0.0 all-gather.2.cloned.1.call-start
  6.5 3.0 convert_reduce_fusion.2
  9.6 79.6 %psum.23 = f32[]{:T(128)} all-reduce(f32[]{:T(128)} %get-tuple-element.7), channel_id=1, replica_groups=mesh['cell'=16,'gene'=16] {'cell','gene'}, use_global_device_ids=true, to_apply=%region_5.0 | all-reduce | flops 1 | bytes 8 | tf_op jit(solution)/shard_map/psum | solution.py:14
  89.1 33.6 %psum.21 = f32[1024]{0:T(1024)S(1)} all-reduce(f32[1024]{0:T(1024)S(1)} %get-tuple-element.5), channel_id=1, replica_groups=mesh['cell'=16,'gene'=16] {'gene'}, use_global_device_ids=true, to_apply=%region_1.0 | all-reduce | flops 1024 | bytes 8192 | tf_op jit(solution)/shard_map/psum | solution.py:12
  122.7 34.4 %psum.22 = f32[512]{0:T(512)S(1)} all-reduce(f32[512]{0:T(512)S(1)} %get-tuple-element.6), channel_id=1, replica_groups=mesh['cell'=16,'gene'=16] {'cell'}, use_global_device_ids=true, to_apply=%region_3.0 | all-reduce | flops 512 | bytes 4096 | tf_op jit(solution)/shard_map/psum | solution.py:13
  157.1 0.0 copy-done
  157.1 2.4 clamp_convert_fusion
  159.5 0.0 all-gather.2.cloned.1.call-update
  159.5 0.0 reduce-scatter.2.cloned.1.call-start
  159.6 194.0 %all-gather.2.cloned.1.call-done = bf16[1024,8192]{1,0:T(8,128)(2,1)} async-done(((bf16[1024,512]{1,0:T(8,128)(2,1)}), bf16[1024,8192]{1,0:T(8,128)(2,1)}) %all-gather.2.cloned.1.call-update) | async-done | bytes 16777232 | tf_op jit(solution)/shard_map/all_gather | solution.py:19
  353.6 16.0 %fusion = f32[8192,512]{1,0:T(8,128)} fusion(bf16[1024,8192]{1,0:T(8,128)(2,1)} %all-gather.2.cloned.1.call-done, bf16[1024,512]{1,0:T(8,128)(2,1)} %clamp_convert_fusion), kind=kOutput, calls=%fused_computation.5 | convolution fusion | flops 8589934592 | bytes 34603008 | tf_op jit(solution)/shard_map/dot_general | solution.py:21
  369.6 0.0 reduce-scatter.2.cloned.1.call-update
  369.6 107.2 %reduce-scatter.2.cloned.1.call-done = f32[512,512]{1,0:T(8,128)} async-done(((f32[8192,512]{1,0:T(8,128)}), f32[512,512]{1,0:T(8,128)}) %reduce-scatter.2.cloned.1.call-update) | async-done | bytes 1048592 | tf_op jit(solution)/shard_map/reduce_scatter | solution.py:20
  476.8 1.3 multiply_bitcast_fusion
  478.1 1.3 copy.2
Async XLA Ops:
  6.5 150.5 %copy-start = (s32[1024,512]{1,0:T(8,128)S(1)}, s32[1024,512]{1,0:T(8,128)}, u32[]{:S(2)}) copy-start(s32[1024,512]{1,0:T(8,128)} %param.1) | copy-start | bytes 6291460
  6.5 347.1 %all-gather.2.cloned.1.call-start = ((), (), s32[]{:S(2)}) async-start(), calls=%async_computation.1 | async-start | bytes 17825792 | tf_op jit(solution)/shard_map/all_gather | solution.py:19
  159.5 317.3 %reduce-scatter.2.cloned.1.call-start = ((), (), s32[]{:S(2)}) async-start(), calls=%async_computation.2 | async-start | bytes 17825792 | tf_op jit(solution)/shard_map/reduce_scatter | solution.py:20
Sparse Core Ops, SparseCore 0:
  159.7 193.8 all-gather.1
  369.7 107.0 reduce-scatter.1
where the time goes:
time: 488 us; the launch traced here: 486 us
  waiting for transfers between devices  301 us (62%)
  blocking collectives  148 us (30%)
  matrix products  16 us (3%)
  between operations  13.4 us (3%)
  other arithmetic  6.77 us (1%)
    all_gather x1, waiting for transfers between devices, body(): gathered = lax.all_gather(residuals, 'gene', axis=1, tiled=True)  194 us
    reduce_scatter x1, waiting for transfers between devices, body(): lax.psum_scatter(lax.dot_general(gathered, residuals, (((0,), (0,)), ((),...  107 us
    psum x1, blocking collectives, body(): grand_total = lax.psum(jnp.sum(row_part), ('cell', 'gene'))  79.6 us
    psum x1, blocking collectives, body(): gene_totals = lax.psum(column_part, 'cell')  34.4 us
    psum x1, blocking collectives, body(): depths = lax.psum(row_part, 'gene')  33.6 us
    dot_general x1, matrix products, body(): lax.dot_general(gathered, residuals, (((0,), (0,)), ((), ())), preferred_...  16 us
  transfers between devices with their start and end apart: 2, of which 2 were waited for; matrix products, arithmetic and copies ran while one was open for 0% of the time, Pallas kernels for 0%

commit v1 on v0

v1 whole, which is shorter than its diff:
```python
import functools

import jax
import jax.numpy as jnp
from jax import lax
from jax.experimental import pallas as pl
from jax.experimental.pallas import tpu as pltpu
from jax.sharding import PartitionSpec as P

MESH = pl.DeviceIdType.MESH
R = 4
NC = 16
YP, ZP, T, Y2, ZM = range(5)
OWN = -1
OFFSET = {OWN: (0, 0), YP: (1, 0), ZP: (0, 1), T: (3, 3), Y2: (2, 3), ZM: (0, 3)}
OWN_PAIRS = (YP, ZP, T, Y2)
PAIRS = (
    (OWN, OWN, False),
    (OWN, YP, True),
    (OWN, ZP, True),
    (OWN, T, True),
    (OWN, Y2, True),
    (YP, ZP, True),
    (ZM, Y2, False),
    (ZP, T, True),
    (ZP, Y2, False),
    (ZP, ZM, False),
)
MIRRORED = ((3, 0), (0, 3), (1, 1), (2, 1), (1, 3), (1, 2))


def plan():
    rounds = []
    for r in range(R):
        groups, n = [], 0

        def add(pair, count, i, j, along):
            nonlocal n
            groups.append((pair, n, count, i, j, along))
            n += count

        if r == 0:
            for i in range(R):
                add(0, R, i, 0, "j")
        for pair in range(1, 5):
            add(pair, R, 0, r, "i")
        for pair in range(5, 10):
            add(pair, r + 1, r, 0, "j")
            if r:
                add(pair, r, 0, r, "i")
        rounds.append((n, groups))
    return rounds


ROUNDS = plan()


def gene_at(y, z, offset):
    return ((y + offset[0]) % 4) * 4 + (z + offset[1]) % 4


def kernel(counts, out, *scratch):
    (vt, colbuf, rowbuf, totbuf, own, got, final), rest = scratch[:7], scratch[7:]
    prods, rest = rest[:R], rest[R:]
    halves, rest = rest[:R], rest[R:]
    early, rest = rest[:R], rest[R:]
    late, rest = rest[:R], rest[R:]
    pieces, rest = rest[:R], rest[R:]
    (stat_send, stat_recv, in_send, in_recv, rs_send, rs_recv, fin_send, fin_own, fin_recv) = rest
    genes, cells = own.shape[0] * own.shape[1], own.shape[2]
    S = genes // R
    nj = cells // 128
    c, g = lax.axis_index("cell"), lax.axis_index("gene")
    zl, x, core = c // 8, (c // 2) % 4, c % 2
    y, z = g // 4, g % 4
    pos = 8 * core + 2 * x + zl

    def cell_of(zl_, x_, core_):
        return {"cell": zl_ * 8 + x_ * 2 + core_}

    xp, xm = (x + 1) % 4, (x + 3) % 4
    to_xp, to_xm = cell_of(zl, xp, core), cell_of(zl, xm, core)
    to_core, to_zl = cell_of(zl, x, 1 - core), cell_of(1 - zl, x, core)
    to_yp, to_ym = {"gene": gene_at(y, z, (1, 0))}, {"gene": gene_at(y, z, (3, 0))}
    to_zp, to_zm = {"gene": gene_at(y, z, (0, 1))}, {"gene": gene_at(y, z, (0, 3))}

    def remote(src, dst, ssem, rsem, device):
        return pltpu.make_async_remote_copy(
            src_ref=src, dst_ref=dst, send_sem=ssem, recv_sem=rsem, device_id=device, device_id_type=MESH
        )

    barrier = pltpu.get_barrier_semaphore()
    for k in range(1, NC):
        pl.semaphore_signal(barrier, inc=1, device_id={"cell": (c + k) % NC}, device_id_type=MESH)
        pl.semaphore_signal(barrier, inc=1, device_id={"gene": (g + k) % NC}, device_id_type=MESH)

    def local(j, acc):
        v = counts[pl.ds(j * 128, 128), :].astype(jnp.float32)
        t = v.T
        vt[j] = t
        rowbuf[g, pl.ds(j, 1), :] = jnp.sum(t, axis=0, keepdims=True)
        return acc + jnp.sum(v, axis=0, keepdims=True)

    nq = genes // 128
    colsum = lax.fori_loop(0, nj, local, jnp.zeros((1, genes), jnp.float32))
    colbuf[c] = jnp.zeros((8, 128), jnp.float32)
    for q in range(nq):
        colbuf[c, q : q + 1, :] = colsum[:, q * 128 : (q + 1) * 128]
    pl.semaphore_wait(barrier, 2 * (NC - 1))

    def spread(buf, axis, me, k):
        for d in range(1, NC):
            remote(buf.at[me], buf.at[me], stat_send.at[k], stat_recv.at[k], {axis: (me + d) % NC}).start()

    def others(buf, sem):
        return pltpu.make_async_copy(buf.at[0 : NC - 1], buf.at[0 : NC - 1], sem)

    spread(colbuf, "cell", c, 0)
    spread(rowbuf, "gene", g, 1)
    others(colbuf, stat_recv.at[0]).wait()
    totals = jnp.sum(colbuf[...], axis=0)
    totbuf[g] = jnp.broadcast_to(jnp.sum(totals, axis=0, keepdims=True), (8, 128))
    spread(totbuf, "gene", g, 2)
    gcol = [jnp.broadcast_to(totals[q : q + 1, :], (128, 128)).T for q in range(nq)]
    others(rowbuf, stat_recv.at[1]).wait()
    depths = jnp.sum(rowbuf[...], axis=0)
    others(totbuf, stat_recv.at[2]).wait()
    grand = jnp.sum(jnp.sum(totbuf[...], axis=0)[0:1, :])
    share = depths / grand
    ceiling = float(NC * cells) ** 0.5
    for q in range(nq):
        r, o = (q * 128) // S, (q * 128) % S
        for j in range(nj):
            v = vt[j, q * 128 : (q + 1) * 128, :]
            e = gcol[q] * share[j : j + 1, :]
            s = (v - e) * lax.rsqrt(e + e * e / 100.0)
            own[r, o : o + 128, j * 128 : (j + 1) * 128] = jnp.clip(s, -ceiling, ceiling).astype(jnp.bfloat16)

    def chunk(src, r, b, device):
        return remote(src, got.at[r, b], in_send.at[b, r], in_recv.at[b, r], device)

    def own_to(b, r, device):
        return chunk(own.at[r], r, b, device)

    def relay(a, b, r, device):
        return chunk(got.at[r, a], r, b, device)

    for r in range(R):
        own_to(ZM, r, to_zp).start()
        own_to(ZP, r, to_zm).start()
        if r < 1:
            own_to(YP, r, to_ym).start()

    def arrived(b, r):
        own_to(b, r, to_zp).wait_recv()

    def nt(a, b):
        return lax.dot_general(a, b, (((1,), (1,)), ((), ())), preferred_element_type=jnp.float32)

    def put(r, t, tile):
        prods[r][t] = tile.reshape(8, S // 8, S)

    def compute(r):
        base = {}
        for pair, t0, n, i, j, along in ROUNDS[r][1]:
            base[pair, along, i if along == "j" and pair == 0 else 0] = t0
        if r == 0:

            @pl.loop(0, R)
            def _(i):
                d = nt(own[i], own[...].reshape(genes, cells))
                for j in range(R):
                    put(r, base[0, "j", 0] + i * R + j, d[:, j * S : (j + 1) * S])

        @pl.loop(0, R)
        def _(i):
            d = nt(own[i], got[r, 0:4].reshape(4 * S, cells))
            for k in range(4):
                put(r, base[k + 1, "i", 0] + i, d[:, k * S : (k + 1) * S])

        @pl.loop(0, r + 1)
        def _(j):
            d = nt(got[r, ZP], got[j, T : ZM + 1].reshape(3 * S, cells))
            for k in range(3):
                put(r, base[k + 7, "j", 0] + j, d[:, k * S : (k + 1) * S])
            put(r, base[5, "j", 0] + j, nt(got[r, YP], got[j, ZP]))
            put(r, base[6, "j", 0] + j, nt(got[r, ZM], got[j, Y2]))

        if r:

            @pl.loop(0, r)
            def _(i):
                d = nt(got[i, ZP], got[r, T : ZM + 1].reshape(3 * S, cells))
                for k in range(3):
                    put(r, base[k + 7, "i", 0] + i, d[:, k * S : (k + 1) * S])
                put(r, base[5, "i", 0] + i, nt(got[i, YP], got[r, ZP]))
                put(r, base[6, "i", 0] + i, nt(got[i, ZM], got[r, Y2]))

    def rs(r, k, src, dst, device):
        return remote(src, dst, rs_send.at[r, k], rs_recv.at[r, k], device)

    def core_copy(r):
        return rs(r, 0, prods[r].at[:, pl.ds(4 * (1 - core), 4)], halves[r], to_core)

    def x_copy(r, k):
        n = ROUNDS[r][0]
        a, b, p, h = slice(0, n // 2), slice(n // 2, n), prods[r], 4 * core
        if k == "ep":
            return rs(r, 1, p.at[a, h + (x + 2) % 4], early[r].at[a], to_xp)
        if k == "em":
            return rs(r, 2, p.at[b, h + (x + 2) % 4], early[r].at[b], to_xm)
        if k == "dp":
            return rs(r, 3, p.at[b, h + xp], late[r].at[0, b], to_xp)
        if k == "dm":
            return rs(r, 4, p.at[a, h + xm], late[r].at[1, a], to_xm)
        if k == "fp":
            return rs(r, 5, p.at[a, h + xp], late[r].at[0, a], to_xp)
        return rs(r, 6, p.at[b, h + xm], late[r].at[1, b], to_xm)

    def zl_copy(r):
        s = S // 16
        return rs(r, 7, prods[r].at[:, 4 * core + x, pl.ds((1 - zl) * s, s)], pieces[r], to_zl)

    def s0(r):
        core_copy(r).start()

    def s1(r):
        n = ROUNDS[r][0]
        core_copy(r).wait_recv()

        @pl.loop(0, n)
        def _(t):
            prods[r][t, pl.ds(4 * core, 4)] = prods[r][t, pl.ds(4 * core, 4)] + halves[r][t]

        for k in ("ep", "em", "dp", "dm"):
            x_copy(r, k).start()

    def s2(r):
        n = ROUNDS[r][0]
        a, b = slice(0, n // 2), slice(n // 2, n)
        x_copy(r, "ep").wait_recv()
        prods[r][a, 4 * core + xp] = prods[r][a, 4 * core + xp] + early[r][a]
        x_copy(r, "fp").start()
        x_copy(r, "em").wait_recv()
        prods[r][b, 4 * core + xm] = prods[r][b, 4 * core + xm] + early[r][b]
        x_copy(r, "fm").start()

    def s3(r):
        for k in ("dp", "dm", "fp", "fm"):
            x_copy(r, k).wait_recv()
        prods[r][:, 4 * core + x] = prods[r][:, 4 * core + x] + late[r][0] + late[r][1]
        zl_copy(r).start()

    def final_sends(r):
        for pair, t0, n, i, j, along in ROUNDS[r][1]:
            a, b, both = PAIRS[pair]
            ga, gb = gene_at(y, z, OFFSET[a]), gene_at(y, z, OFFSET[b])
            if along == "j":
                dst = final.at[i, j : j + n, pos]
            else:
                dst = final.at[i : i + n, j, pos]
            yield pieces[r].at[t0 : t0 + n], dst, ga, gb, a == OWN
            if both:
                yield pieces[r].at[t0 : t0 + n], dst, gb, ga, False

    def s4(r):
        s = S // 16
        zl_copy(r).wait_recv()
        pieces[r][...] = pieces[r][...] + prods[r][:, 4 * core + x, pl.ds(zl * s, s)]
        k = 0
        for src, dst, row, col, maybe in final_sends(r):
            if maybe:

                @pl.when(col == c)
                def _():
                    pltpu.make_async_copy(src, dst, fin_recv).start()

                @pl.when(col != c)
                def _():
                    remote(src, dst, fin_own.at[r, k], fin_recv, {"cell": col, "gene": row}).start()

                k += 1
            else:
                remote(src, dst, fin_send, fin_recv, {"cell": col, "gene": row}).start()

    arrived(ZM, 0)
    relay(ZM, T, 0, to_yp).start()
    for r in range(R):
        if r + 1 < R:
            own_to(YP, r + 1, to_ym).start()
        arrived(T, r)
        relay(T, Y2, r, to_yp).start()
        if r + 1 < R:
            arrived(ZM, r + 1)
            relay(ZM, T, r + 1, to_yp).start()
        arrived(ZP, r)
        arrived(YP, r)
        arrived(Y2, r)
        compute(r)
        s0(r)
        if r:
            s3(r - 1)
        s1(r)
        if r:
            s4(r - 1)
        s2(r)
    s3(R - 1)
    s4(R - 1)

    pltpu.make_async_copy(final, final, fin_recv).wait()
    dy, dz = (c // 4 - y + 4) % 4, (c % 4 - z + 4) % 4
    flip = functools.reduce(jnp.logical_or, [(dy == a) & (dz == b) for a, b in MIRRORED])
    scale = 1.0 / float(NC * cells)

    def tile(i, j):
        return final[i, j].reshape(S, S) * scale

    @pl.when(flip)
    def _():
        for i in range(R):
            for j in range(R):
                out[j * S : (j + 1) * S, i * S : (i + 1) * S] = tile(i, j).T

    @pl.when(jnp.logical_not(flip))
    def _():
        for i in range(R):
            for j in range(R):
                out[i * S : (i + 1) * S, j * S : (j + 1) * S] = tile(i, j)

    for k, buf in ((0, colbuf), (1, rowbuf), (2, totbuf)):
        others(buf, stat_send.at[k]).wait()
    sent = 0
    for r in range(R):
        for b in range(5):
            own_to(b, r, to_zp).wait_send()
        core_copy(r).wait_send()
        for k in ("ep", "em", "dp", "dm", "fp", "fm"):
            x_copy(r, k).wait_send()
        zl_copy(r).wait_send()
        k = 0
        for src, dst, row, col, maybe in final_sends(r):
            if maybe:

                @pl.when(col != c)
                def _():
                    remote(src, dst, fin_own.at[r, k], fin_recv, {"cell": col, "gene": row}).wait_send()

                k += 1
            else:
                sent += src.shape[0]
    assert sent % 16 == 0
    pltpu.make_async_copy(prods[0].at[0 : sent // 16], prods[0].at[0 : sent // 16], fin_send).wait()


def body(counts):
    cells, genes = counts.shape
    S = genes // R
    ns = [n for n, _ in ROUNDS]
    f32 = jnp.float32
    dma = pltpu.SemaphoreType.DMA
    own_groups = max(sum(PAIRS[gr[0]][0] == OWN for gr in groups) for _, groups in ROUNDS)
    scratch = [
        pltpu.VMEM((cells // 128, genes, 128), f32),
        pltpu.VMEM((NC, 8, 128), f32),
        pltpu.VMEM((NC, 8, 128), f32),
        pltpu.VMEM((NC, 8, 128), f32),
        pltpu.VMEM((R, S, cells), jnp.bfloat16),
        pltpu.VMEM((R, 5, S, cells), jnp.bfloat16),
        pltpu.VMEM((R, R, 16, S // 16, S), f32),
        *[pltpu.VMEM((n, 8, S // 8, S), f32) for n in ns],
        *[pltpu.VMEM((n, 4, S // 8, S), f32) for n in ns],
        *[pltpu.VMEM((n, S // 8, S), f32) for n in ns],
        *[pltpu.VMEM((2, n, S // 8, S), f32) for n in ns],
        *[pltpu.VMEM((n, S // 16, S), f32) for n in ns],
        dma((3,)),
        dma((3,)),
        dma((5, R)),
        dma((5, R)),
        dma((R, 8)),
        dma((R, 8)),
        dma(()),
        dma((R, own_groups)),
        dma(()),
    ]
    return pl.pallas_call(
        kernel,
        out_shape=jax.ShapeDtypeStruct((genes, genes), f32),
        in_specs=[pl.BlockSpec(memory_space=pltpu.VMEM)],
        out_specs=pl.BlockSpec(memory_space=pltpu.VMEM),
        scratch_shapes=scratch,
        compiler_params=pltpu.CompilerParams(
            collective_id=0, has_side_effects=True, vmem_limit_bytes=60 * 1024 * 1024
        ),
    )(counts)


def solution(mesh):
    return jax.shard_map(
        body,
        mesh=mesh,
        in_specs=(P("cell", "gene"),),
        out_specs=P("gene", "cell"),
        check_vma=False,
    )
```

time: 488 us -> 176 us (0.36)
  waiting for transfers between devices: 301 us -> 0 us
  Pallas kernels: 0 us -> 174 us
  blocking collectives: 148 us -> 0 us
  matrix products: 16 us -> 0 us
  between operations: 13.4 us -> 0.01 us
  other arithmetic: 6.77 us -> 0 us
    all_gather x1 -> x0, waiting for transfers between devices: 194 us -> none  [body(): gathered = lax.all_gather(residuals, 'gene', axis=1, tiled=True)]
    pallas_call x0 -> x1, Pallas kernels: none -> 174 us  [body(): pl.pallas_call(kernel, out_shape=jax.ShapeDtypeStruct((genes, genes), f32...]
    psum x3 -> x0, blocking collectives: 148 us -> none  [the longest x1 79.6 us: body(): grand_total = lax.psum(jnp.sum(row_part), ('cell', 'gene'))]
    reduce_scatter x1 -> x0, waiting for transfers between devices: 107 us -> none  [body(): lax.psum_scatter(lax.dot_general(gathered, residuals, (((0,), (0,)), ((),...]
    dot_general x1 -> x0, matrix products: 16 us -> none  [body(): lax.dot_general(gathered, residuals, (((0,), (0,)), ((), ())), preferred_...]
  transfers between devices with their start and end apart: 2 -> 0, of which waited for: 2 -> 0; matrix products, arithmetic and copies ran while one was open for 0% -> 0% of each run, Pallas kernels for 0% -> 0%
where the time goes in v1:
time: 176 us
  Pallas kernels  174 us (99%)
  local copies, waits for them, and re-layouts  2.26 us (1%)
    pallas_call x1, Pallas kernels, body(): pl.pallas_call(kernel, out_shape=jax.ShapeDtypeStruct((genes, genes), f32...  174 us

profile of v1, /device:TPU:33, one launch (start us, length us, event | category | flops | bytes accessed | tf_op | source)
XLA Modules:
  0.0 175.9 jit_solution(12534630834874291763)
XLA Ops:
  0.0 173.7 %shard_map.17 = f32[512,512]{1,0:T(8,128)} custom-call(s32[1024,512]{1,0:T(8,128)} %counts.1), custom_call_target="tpu_custom_call" | custom-call | tf_op jit(solution)/shard_map/pallas_call | solution.py:385
  173.7 2.3 %copy.3 = f32[512,512]{1,0:T(8,128)} copy(f32[512,512]{1,0:T(8,128)} %shard_map.17) | data formatting | bytes 2097152

commit v2 on v1

--- a/solution.py
+++ b/solution.py
@@ -13,7 +13,6 @@
 YP, ZP, T, Y2, ZM = range(5)
 OWN = -1
 OFFSET = {OWN: (0, 0), YP: (1, 0), ZP: (0, 1), T: (3, 3), Y2: (2, 3), ZM: (0, 3)}
-OWN_PAIRS = (YP, ZP, T, Y2)
 PAIRS = (
     (OWN, OWN, False),
     (OWN, YP, True),
@@ -29,9 +28,13 @@
 MIRRORED = ((3, 0), (0, 3), (1, 1), (2, 1), (1, 3), (1, 2))
 
 
+EARLY_OWN, EARLY_BOTH = (1, 2), (5, 9)
+LATE_OWN, LATE_BOTH = (3, 4), (6, 7, 8)
+
+
 def plan():
-    rounds = []
-    for r in range(R):
+    batches = []
+    for step in range(-1, R + 1):
         groups, n = [], 0
 
         def add(pair, count, i, j, along):
@@ -39,20 +42,23 @@
             groups.append((pair, n, count, i, j, along))
             n += count
 
-        if r == 0:
+        if step < 0:
             for i in range(R):
                 add(0, R, i, 0, "j")
-        for pair in range(1, 5):
-            add(pair, R, 0, r, "i")
-        for pair in range(5, 10):
-            add(pair, r + 1, r, 0, "j")
-            if r:
-                add(pair, r, 0, r, "i")
-        rounds.append((n, groups))
-    return rounds
+        for r, alone, both in ((step, EARLY_OWN, EARLY_BOTH), (step - 1, LATE_OWN, LATE_BOTH)):
+            if 0 <= r < R:
+                for pair in alone:
+                    add(pair, R, 0, r, "i")
+                for pair in both:
+                    add(pair, r + 1, r, 0, "j")
+                    if r:
+                        add(pair, r, 0, r, "i")
+        batches.append((n, groups))
+    return batches
 
 
 ROUNDS = plan()
+NB = len(ROUNDS)
 
 
 def gene_at(y, z, offset):
@@ -61,11 +67,11 @@
 
 def kernel(counts, out, *scratch):
     (vt, colbuf, rowbuf, totbuf, own, got, final), rest = scratch[:7], scratch[7:]
-    prods, rest = rest[:R], rest[R:]
-    halves, rest = rest[:R], rest[R:]
-    early, rest = rest[:R], rest[R:]
-    late, rest = rest[:R], rest[R:]
-    pieces, rest = rest[:R], rest[R:]
+    prods, rest = rest[:NB], rest[NB:]
+    halves, rest = rest[:NB], rest[NB:]
+    early, rest = rest[:NB], rest[NB:]
+    late, rest = rest[:NB], rest[NB:]
+    pieces, rest = rest[:NB], rest[NB:]
     (stat_send, stat_recv, in_send, in_recv, rs_send, rs_recv, fin_send, fin_own, fin_recv) = rest
     genes, cells = own.shape[0] * own.shape[1], own.shape[2]
     S = genes // R
@@ -82,6 +88,7 @@
     to_xp, to_xm = cell_of(zl, xp, core), cell_of(zl, xm, core)
     to_core, to_zl = cell_of(zl, x, 1 - core), cell_of(1 - zl, x, core)
     to_yp, to_ym = {"gene": gene_at(y, z, (1, 0))}, {"gene": gene_at(y, z, (3, 0))}
+    to_y2 = {"gene": gene_at(y, z, (2, 0))}
     to_zp, to_zm = {"gene": gene_at(y, z, (0, 1))}, {"gene": gene_at(y, z, (0, 3))}
 
     def remote(src, dst, ssem, rsem, device):
@@ -160,41 +167,63 @@
     def put(r, t, tile):
         prods[r][t] = tile.reshape(8, S // 8, S)
 
-    def compute(r):
+    def compute(m):
         base = {}
-        for pair, t0, n, i, j, along in ROUNDS[r][1]:
-            base[pair, along, i if along == "j" and pair == 0 else 0] = t0
-        if r == 0:
+        for pair, t0, n, i, j, along in ROUNDS[m][1]:
+            base.setdefault((pair, along), t0)
+        if m == 0:
 
             @pl.loop(0, R)
             def _(i):
                 d = nt(own[i], own[...].reshape(genes, cells))
                 for j in range(R):
-                    put(r, base[0, "j", 0] + i * R + j, d[:, j * S : (j + 1) * S])
-
-        @pl.loop(0, R)
-        def _(i):
-            d = nt(own[i], got[r, 0:4].reshape(4 * S, cells))
-            for k in range(4):
-                put(r, base[k + 1, "i", 0] + i, d[:, k * S : (k + 1) * S])
-
-        @pl.loop(0, r + 1)
-        def _(j):
-            d = nt(got[r, ZP], got[j, T : ZM + 1].reshape(3 * S, cells))
-            for k in range(3):
-                put(r, base[k + 7, "j", 0] + j, d[:, k * S : (k + 1) * S])
-            put(r, base[5, "j", 0] + j, nt(got[r, YP], got[j, ZP]))
-            put(r, base[6, "j", 0] + j, nt(got[r, ZM], got[j, Y2]))
-
-        if r:
-
-            @pl.loop(0, r)
+                    put(m, i * R + j, d[:, j * S : (j + 1) * S])
+
+            return
+        e, l = m - 1, m - 2
+        if e < R:
+
+            @pl.loop(0, R)
             def _(i):
-                d = nt(got[i, ZP], got[r, T : ZM + 1].reshape(3 * S, cells))
-                for k in range(3):
-                    put(r, base[k + 7, "i", 0] + i, d[:, k * S : (k + 1) * S])
-                put(r, base[5, "i", 0] + i, nt(got[i, YP], got[r, ZP]))
-                put(r, base[6, "i", 0] + i, nt(got[i, ZM], got[r, Y2]))
+                d = nt(own[i], got[e, YP : ZP + 1].reshape(2 * S, cells))
+                for k in range(2):
+                    put(m, base[k + 1, "i"] + i, d[:, k * S : (k + 1) * S])
+
+            @pl.loop(0, e + 1)
+            def _(j):
+                put(m, base[5, "j"] + j, nt(got[e, YP], got[j, ZP]))
+                put(m, base[9, "j"] + j, nt(got[e, ZP], got[j, ZM]))
+
+            if e:
+
+                @pl.loop(0, e)
+                def _(i):
+                    put(m, base[5, "i"] + i, nt(got[i, YP], got[e, ZP]))
+                    put(m, base[9, "i"] + i, nt(got[i, ZP], got[e, ZM]))
+
+        if l >= 0:
+
+            @pl.loop(0, R)
+            def _(i):
+                d = nt(own[i], got[l, T : Y2 + 1].reshape(2 * S, cells))
+                for k in range(2):
+                    put(m, base[k + 3, "i"] + i, d[:, k * S : (k + 1) * S])
+
+            @pl.loop(0, l + 1)
+            def _(j):
+                d = nt(got[l, ZP], got[j, T : Y2 + 1].reshape(2 * S, cells))
+                for k in range(2):
+                    put(m, base[k + 7, "j"] + j, d[:, k * S : (k + 1) * S])
+                put(m, base[6, "j"] + j, nt(got[l, ZM], got[j, Y2]))
+
+            if l:
+
+                @pl.loop(0, l)
+                def _(i):
+                    d = nt(got[i, ZP], got[l, T : Y2 + 1].reshape(2 * S, cells))
+                    for k in range(2):
+                        put(m, base[k + 7, "i"] + i, d[:, k * S : (k + 1) * S])
+                    put(m, base[6, "i"] + i, nt(got[i, ZM], got[l, Y2]))
 
     def rs(r, k, src, dst, device):
         return remote(src, dst, rs_send.at[r, k], rs_recv.at[r, k], device)
@@ -283,29 +312,34 @@
             else:
                 remote(src, dst, fin_send, fin_recv, {"cell": col, "gene": row}).start()
 
-    arrived(ZM, 0)
-    relay(ZM, T, 0, to_yp).start()
-    for r in range(R):
-        if r + 1 < R:
-            own_to(YP, r + 1, to_ym).start()
-        arrived(T, r)
-        relay(T, Y2, r, to_yp).start()
-        if r + 1 < R:
-            arrived(ZM, r + 1)
-            relay(ZM, T, r + 1, to_yp).start()
-        arrived(ZP, r)
-        arrived(YP, r)
-        arrived(Y2, r)
-        compute(r)
-        s0(r)
-        if r:
-            s3(r - 1)
-        s1(r)
-        if r:
-            s4(r - 1)
-        s2(r)
-    s3(R - 1)
-    s4(R - 1)
+    compute(0)
+    s0(0)
+    s1(0)
+    s2(0)
+    for k in range(R + 1):
+        m = k + 1
+        if k < R:
+            arrived(ZM, k)
+            relay(ZM, T, k, to_yp).start()
+            relay(ZM, Y2, k, to_y2).start()
+            if k + 1 < R:
+                own_to(YP, k + 1, to_ym).start()
+        if k:
+            arrived(T, k - 1)
+            arrived(Y2, k - 1)
+        if k < R:
+            arrived(ZP, k)
+            arrived(YP, k)
+        compute(m)
+        s0(m)
+        s1(m)
+        s3(m - 1)
+        s2(m)
+    for m in range(NB - 2):
+        s4(m)
+    s3(NB - 1)
+    s4(NB - 2)
+    s4(NB - 1)
 
     pltpu.make_async_copy(final, final, fin_recv).wait()
     dy, dz = (c // 4 - y + 4) % 4, (c % 4 - z + 4) % 4
@@ -333,6 +367,7 @@
     for r in range(R):
         for b in range(5):
             own_to(b, r, to_zp).wait_send()
+    for r in range(NB):
         core_copy(r).wait_send()
         for k in ("ep", "em", "dp", "dm", "fp", "fm"):
             x_copy(r, k).wait_send()
@@ -376,10 +411,10 @@
         dma((3,)),
         dma((5, R)),
         dma((5, R)),
-        dma((R, 8)),
-        dma((R, 8)),
+        dma((NB, 8)),
+        dma((NB, 8)),
         dma(()),
-        dma((R, own_groups)),
+        dma((NB, own_groups)),
         dma(()),
     ]
     return pl.pallas_call(

time: 176 us -> 166 us (0.943)
  the two profiles are of different devices: /device:TPU:33 before, /device:TPU:34 now
where the time goes in v2:
time: 166 us; the launch traced here: 165 us
  Pallas kernels  163 us (98%)
  local copies, waits for them, and re-layouts  2.26 us (1%)
    pallas_call x1, Pallas kernels, body(): pl.pallas_call(kernel, out_shape=jax.ShapeDtypeStruct((genes, genes), f32...  163 us

profile of v2, /device:TPU:34, one launch (start us, length us, event | category | flops | bytes accessed | tf_op | source)
XLA Modules:
  0.0 165.4 jit_solution(14594053092877720171)
XLA Ops:
  0.0 163.1 %shard_map.17 = f32[512,512]{1,0:T(8,128)} custom-call(s32[1024,512]{1,0:T(8,128)} %counts.1), custom_call_target="tpu_custom_call" | custom-call | tf_op jit(solution)/shard_map/pallas_call | solution.py:420
  163.2 2.3 %copy.3 = f32[512,512]{1,0:T(8,128)} copy(f32[512,512]{1,0:T(8,128)} %shard_map.17) | data formatting | bytes 2097152

commit v3 on v2

--- a/solution.py
+++ b/solution.py
@@ -9,6 +9,7 @@
 
 MESH = pl.DeviceIdType.MESH
 R = 4
+H = 2
 NC = 16
 YP, ZP, T, Y2, ZM = range(5)
 OWN = -1
@@ -143,23 +144,32 @@
             s = (v - e) * lax.rsqrt(e + e * e / 100.0)
             own[r, o : o + 128, j * 128 : (j + 1) * 128] = jnp.clip(s, -ceiling, ceiling).astype(jnp.bfloat16)
 
-    def chunk(src, r, b, device):
-        return remote(src, got.at[r, b], in_send.at[b, r], in_recv.at[b, r], device)
-
-    def own_to(b, r, device):
-        return chunk(own.at[r], r, b, device)
-
-    def relay(a, b, r, device):
-        return chunk(got.at[r, a], r, b, device)
+    def part(h):
+        return slice(h * (S // H), (h + 1) * (S // H))
+
+    def own_to(b, r, h, device):
+        return remote(own.at[r, part(h)], got.at[r, b, part(h)], in_send.at[b, r, h], in_recv.at[b, r, h], device)
+
+    def arrived(b, r, h):
+        own_to(b, r, h, to_zp).wait_recv()
+
+    def pass_on(k, h):
+        arrived(ZM, k, h)
+        src = got.at[k, ZM, part(h)]
+        for b, device in ((T, to_yp), (Y2, to_y2)):
+            remote(src, got.at[k, b, part(h)], in_send.at[b, k, h], in_recv.at[b, k, h], device).start()
+
+    def have(b, r):
+        for h in range(H):
+            arrived(b, r, h)
 
     for r in range(R):
-        own_to(ZM, r, to_zp).start()
-        own_to(ZP, r, to_zm).start()
+        for h in range(H):
+            own_to(ZM, r, h, to_zp).start()
+            own_to(ZP, r, h, to_zm).start()
         if r < 1:
-            own_to(YP, r, to_ym).start()
-
-    def arrived(b, r):
-        own_to(b, r, to_zp).wait_recv()
+            for h in range(H):
+                own_to(YP, r, h, to_ym).start()
 
     def nt(a, b):
         return lax.dot_general(a, b, (((1,), (1,)), ((), ())), preferred_element_type=jnp.float32)
@@ -316,29 +326,34 @@
     s0(0)
     s1(0)
     s2(0)
+    pass_on(0, 0)
     for k in range(R + 1):
         m = k + 1
         if k < R:
-            arrived(ZM, k)
-            relay(ZM, T, k, to_yp).start()
-            relay(ZM, Y2, k, to_y2).start()
+            for h in range(1, H):
+                pass_on(k, h)
             if k + 1 < R:
-                own_to(YP, k + 1, to_ym).start()
+                for h in range(H):
+                    own_to(YP, k + 1, h, to_ym).start()
         if k:
-            arrived(T, k - 1)
-            arrived(Y2, k - 1)
+            have(T, k - 1)
+            have(Y2, k - 1)
         if k < R:
-            arrived(ZP, k)
-            arrived(YP, k)
+            have(ZP, k)
+            have(YP, k)
         compute(m)
         s0(m)
         s1(m)
+        if k + 1 < R:
+            pass_on(k + 1, 0)
         s3(m - 1)
         s2(m)
-    for m in range(NB - 2):
-        s4(m)
+        if k == R - 1:
+            for early_m in range(m - 1):
+                s4(early_m)
+    s4(NB - 3)
+    s4(NB - 2)
     s3(NB - 1)
-    s4(NB - 2)
     s4(NB - 1)
 
     pltpu.make_async_copy(final, final, fin_recv).wait()
@@ -366,7 +381,8 @@
     sent = 0
     for r in range(R):
         for b in range(5):
-            own_to(b, r, to_zp).wait_send()
+            for h in range(H):
+                own_to(b, r, h, to_zp).wait_send()
     for r in range(NB):
         core_copy(r).wait_send()
         for k in ("ep", "em", "dp", "dm", "fp", "fm"):
@@ -409,8 +425,8 @@
         *[pltpu.VMEM((n, S // 16, S), f32) for n in ns],
         dma((3,)),
         dma((3,)),
-        dma((5, R)),
-        dma((5, R)),
+        dma((5, R, H)),
+        dma((5, R, H)),
         dma((NB, 8)),
         dma((NB, 8)),
         dma(()),

time: 166 us -> 162 us (0.976)
  the two profiles are of different devices: /device:TPU:34 before, /device:TPU:33 now
where the time goes in v3:
time: 162 us
  Pallas kernels  159 us (98%)
  local copies, waits for them, and re-layouts  2.26 us (1%)
    pallas_call x1, Pallas kernels, body(): pl.pallas_call(kernel, out_shape=jax.ShapeDtypeStruct((genes, genes), f32...  159 us

profile of v3, /device:TPU:33, one launch (start us, length us, event | category | flops | bytes accessed | tf_op | source)
XLA Modules:
  0.0 161.5 jit_solution(11955173362214221983)
XLA Ops:
  0.0 159.3 %shard_map.17 = f32[512,512]{1,0:T(8,128)} custom-call(s32[1024,512]{1,0:T(8,128)} %counts.1), custom_call_target="tpu_custom_call" | custom-call | tf_op jit(solution)/shard_map/pallas_call | solution.py:436
  159.3 2.3 %copy.3 = f32[512,512]{1,0:T(8,128)} copy(f32[512,512]{1,0:T(8,128)} %shard_map.17) | data formatting | bytes 2097152

commit v4 on v3

--- a/solution.py
+++ b/solution.py
@@ -15,17 +15,18 @@
 OWN = -1
 OFFSET = {OWN: (0, 0), YP: (1, 0), ZP: (0, 1), T: (3, 3), Y2: (2, 3), ZM: (0, 3)}
 PAIRS = (
-    (OWN, OWN, False),
-    (OWN, YP, True),
-    (OWN, ZP, True),
-    (OWN, T, True),
-    (OWN, Y2, True),
-    (YP, ZP, True),
-    (ZM, Y2, False),
-    (ZP, T, True),
-    (ZP, Y2, False),
-    (ZP, ZM, False),
+    (OWN, OWN, None),
+    (OWN, YP, "all"),
+    (OWN, ZP, "all"),
+    (OWN, T, "all"),
+    (OWN, Y2, "all"),
+    (YP, ZP, "all"),
+    (ZM, Y2, "below"),
+    (ZP, T, "all"),
+    (ZP, Y2, "below"),
+    (ZP, ZM, "below"),
 )
+HALVED = ((2, 0), (0, 2), (2, 2))
 MIRRORED = ((3, 0), (0, 3), (1, 1), (2, 1), (1, 3), (1, 2))
 
 
@@ -45,14 +46,14 @@
 
         if step < 0:
             for i in range(R):
-                add(0, R, i, 0, "j")
+                add(0, i + 1, i, 0, "j")
         for r, alone, both in ((step, EARLY_OWN, EARLY_BOTH), (step - 1, LATE_OWN, LATE_BOTH)):
             if 0 <= r < R:
                 for pair in alone:
                     add(pair, R, 0, r, "i")
                 for pair in both:
                     add(pair, r + 1, r, 0, "j")
-                    if r:
+                    if r and PAIRS[pair][2] == "all":
                         add(pair, r, 0, r, "i")
         batches.append((n, groups))
     return batches
@@ -177,63 +178,59 @@
     def put(r, t, tile):
         prods[r][t] = tile.reshape(8, S // 8, S)
 
-    def compute(m):
+    def base_of(m):
         base = {}
         for pair, t0, n, i, j, along in ROUNDS[m][1]:
             base.setdefault((pair, along), t0)
-        if m == 0:
-
-            @pl.loop(0, R)
+        return base
+
+    def compute_diagonal():
+        for i in range(R):
+            d = nt(own[i], own[0 : i + 1].reshape((i + 1) * S, cells))
+            for j in range(i + 1):
+                put(0, i * (i + 1) // 2 + j, d[:, j * S : (j + 1) * S])
+
+    def compute_early(m):
+        base, e = base_of(m), m - 1
+
+        @pl.loop(0, R)
+        def _(i):
+            d = nt(own[i], got[e, YP : ZP + 1].reshape(2 * S, cells))
+            for k in range(2):
+                put(m, base[k + 1, "i"] + i, d[:, k * S : (k + 1) * S])
+
+        @pl.loop(0, e + 1)
+        def _(j):
+            put(m, base[5, "j"] + j, nt(got[e, YP], got[j, ZP]))
+            put(m, base[9, "j"] + j, nt(got[e, ZP], got[j, ZM]))
+
+        if e:
+
+            @pl.loop(0, e)
             def _(i):
-                d = nt(own[i], own[...].reshape(genes, cells))
-                for j in range(R):
-                    put(m, i * R + j, d[:, j * S : (j + 1) * S])
-
-            return
-        e, l = m - 1, m - 2
-        if e < R:
-
-            @pl.loop(0, R)
+                put(m, base[5, "i"] + i, nt(got[i, YP], got[e, ZP]))
+
+    def compute_late(m):
+        base, l = base_of(m), m - 2
+
+        @pl.loop(0, R)
+        def _(i):
+            d = nt(own[i], got[l, T : Y2 + 1].reshape(2 * S, cells))
+            for k in range(2):
+                put(m, base[k + 3, "i"] + i, d[:, k * S : (k + 1) * S])
+
+        @pl.loop(0, l + 1)
+        def _(j):
+            d = nt(got[l, ZP], got[j, T : Y2 + 1].reshape(2 * S, cells))
+            for k in range(2):
+                put(m, base[k + 7, "j"] + j, d[:, k * S : (k + 1) * S])
+            put(m, base[6, "j"] + j, nt(got[l, ZM], got[j, Y2]))
+
+        if l:
+
+            @pl.loop(0, l)
             def _(i):
-                d = nt(own[i], got[e, YP : ZP + 1].reshape(2 * S, cells))
-                for k in range(2):
-                    put(m, base[k + 1, "i"] + i, d[:, k * S : (k + 1) * S])
-
-            @pl.loop(0, e + 1)
-            def _(j):
-                put(m, base[5, "j"] + j, nt(got[e, YP], got[j, ZP]))
-                put(m, base[9, "j"] + j, nt(got[e, ZP], got[j, ZM]))
-
-            if e:
-
-                @pl.loop(0, e)
-                def _(i):
-                    put(m, base[5, "i"] + i, nt(got[i, YP], got[e, ZP]))
-                    put(m, base[9, "i"] + i, nt(got[i, ZP], got[e, ZM]))
-
-        if l >= 0:
-
-            @pl.loop(0, R)
-            def _(i):
-                d = nt(own[i], got[l, T : Y2 + 1].reshape(2 * S, cells))
-                for k in range(2):
-                    put(m, base[k + 3, "i"] + i, d[:, k * S : (k + 1) * S])
-
-            @pl.loop(0, l + 1)
-            def _(j):
-                d = nt(got[l, ZP], got[j, T : Y2 + 1].reshape(2 * S, cells))
-                for k in range(2):
-                    put(m, base[k + 7, "j"] + j, d[:, k * S : (k + 1) * S])
-                put(m, base[6, "j"] + j, nt(got[l, ZM], got[j, Y2]))
-
-            if l:
-
-                @pl.loop(0, l)
-                def _(i):
-                    d = nt(got[i, ZP], got[l, T : Y2 + 1].reshape(2 * S, cells))
-                    for k in range(2):
-                        put(m, base[k + 7, "i"] + i, d[:, k * S : (k + 1) * S])
-                    put(m, base[6, "i"] + i, nt(got[i, ZM], got[l, Y2]))
+                put(m, base[7, "i"] + i, nt(got[i, ZP], got[l, T]))
 
     def rs(r, k, src, dst, device):
         return remote(src, dst, rs_send.at[r, k], rs_recv.at[r, k], device)
@@ -299,8 +296,10 @@
             else:
                 dst = final.at[i : i + n, j, pos]
             yield pieces[r].at[t0 : t0 + n], dst, ga, gb, a == OWN
-            if both:
+            if both == "all":
                 yield pieces[r].at[t0 : t0 + n], dst, gb, ga, False
+            if both == "below" and i:
+                yield pieces[r].at[t0 : t0 + i], final.at[0:i, i, pos], gb, ga, False
 
     def s4(r):
         s = S // 16
@@ -322,7 +321,7 @@
             else:
                 remote(src, dst, fin_send, fin_recv, {"cell": col, "gene": row}).start()
 
-    compute(0)
+    compute_diagonal()
     s0(0)
     s1(0)
     s2(0)
@@ -335,13 +334,14 @@
             if k + 1 < R:
                 for h in range(H):
                     own_to(YP, k + 1, h, to_ym).start()
+        if k < R:
+            have(ZP, k)
+            have(YP, k)
+            compute_early(m)
         if k:
             have(T, k - 1)
             have(Y2, k - 1)
-        if k < R:
-            have(ZP, k)
-            have(YP, k)
-        compute(m)
+            compute_late(m)
         s0(m)
         s1(m)
         if k + 1 < R:
@@ -349,32 +349,63 @@
         s3(m - 1)
         s2(m)
         if k == R - 1:
-            for early_m in range(m - 1):
-                s4(early_m)
-    s4(NB - 3)
+            for done in range(m):
+                s4(done)
     s4(NB - 2)
     s3(NB - 1)
     s4(NB - 1)
 
-    pltpu.make_async_copy(final, final, fin_recv).wait()
     dy, dz = (c // 4 - y + 4) % 4, (c % 4 - z + 4) % 4
-    flip = functools.reduce(jnp.logical_or, [(dy == a) & (dz == b) for a, b in MIRRORED])
+
+    def among(offsets):
+        return functools.reduce(jnp.logical_or, [(dy == a) & (dz == b) for a, b in offsets])
+
+    diagonal, halved, flip = among(((0, 0),)), among(HALVED), among(MIRRORED)
     scale = 1.0 / float(NC * cells)
+
+    def write(i, j, tile):
+        out[i * S : (i + 1) * S, j * S : (j + 1) * S] = tile
 
     def tile(i, j):
         return final[i, j].reshape(S, S) * scale
 
-    @pl.when(flip)
+    below = [(i, j) for i in range(R) for j in range(i)]
+    above = [(i, j) for j, i in below]
+    even = [(i, i) for i in range(R)]
+
+    @pl.when(diagonal)
     def _():
-        for i in range(R):
-            for j in range(R):
-                out[j * S : (j + 1) * S, i * S : (i + 1) * S] = tile(i, j).T
-
-    @pl.when(jnp.logical_not(flip))
+        lower = prods[0].at[0 : len(below + even)]
+        pltpu.make_async_copy(lower, lower, fin_recv).wait()
+        for i, j in below:
+            write(i, j, tile(i, j))
+            write(j, i, tile(i, j).T)
+        for i, j in even:
+            write(i, j, tile(i, j))
+
+    @pl.when(jnp.logical_not(diagonal))
     def _():
-        for i in range(R):
-            for j in range(R):
-                out[i * S : (i + 1) * S, j * S : (j + 1) * S] = tile(i, j)
+        pltpu.make_async_copy(final, final, fin_recv).wait()
+
+        @pl.when(flip)
+        def _():
+            for i, j in below + even + above:
+                write(j, i, tile(i, j).T)
+
+        @pl.when(jnp.logical_not(flip))
+        def _():
+            for i, j in below + even:
+                write(i, j, tile(i, j))
+
+            @pl.when(halved)
+            def _():
+                for i, j in above:
+                    write(i, j, tile(i, j).T)
+
+            @pl.when(jnp.logical_not(halved))
+            def _():
+                for i, j in above:
+                    write(i, j, tile(i, j))
 
     for k, buf in ((0, colbuf), (1, rowbuf), (2, totbuf)):
         others(buf, stat_send.at[k]).wait()
@@ -400,7 +431,7 @@
             else:
                 sent += src.shape[0]
     assert sent % 16 == 0
-    pltpu.make_async_copy(prods[0].at[0 : sent // 16], prods[0].at[0 : sent // 16], fin_send).wait()
+    pltpu.make_async_copy(prods[2].at[0 : sent // 16], prods[2].at[0 : sent // 16], fin_send).wait()
 
 
 def body(counts):

time: 162 us -> 159 us (0.981)
  Pallas kernels: 159 us -> 155 us
    pallas_call x1, Pallas kernels: 159 us -> 155 us  [body(): pl.pallas_call(kernel, out_shape=jax.ShapeDtypeStruct((genes, genes), f32...]
where the time goes in v4:
time: 159 us; the launch traced here: 158 us
  Pallas kernels  155 us (97%)
  local copies, waits for them, and re-layouts  2.26 us (1%)
    pallas_call x1, Pallas kernels, body(): pl.pallas_call(kernel, out_shape=jax.ShapeDtypeStruct((genes, genes), f32...  155 us

profile of v4, /device:TPU:33, one launch (start us, length us, event | category | flops | bytes accessed | tf_op | source)
XLA Modules:
  0.0 157.7 jit_solution(17606354910153950826)
XLA Ops:
  0.0 155.4 %shard_map.17 = f32[512,512]{1,0:T(8,128)} custom-call(s32[1024,512]{1,0:T(8,128)} %counts.1), custom_call_target="tpu_custom_call" | custom-call | tf_op jit(solution)/shard_map/pallas_call | solution.py:467
  155.4 2.3 %copy.3 = f32[512,512]{1,0:T(8,128)} copy(f32[512,512]{1,0:T(8,128)} %shard_map.17) | data formatting | bytes 2097152

commit v5 on v4

--- a/solution.py
+++ b/solution.py
@@ -68,13 +68,13 @@
 
 
 def kernel(counts, out, *scratch):
-    (vt, colbuf, rowbuf, totbuf, own, got, final), rest = scratch[:7], scratch[7:]
+    (vt, colbuf, rowbuf, totbuf, own, got, mid, final), rest = scratch[:8], scratch[8:]
     prods, rest = rest[:NB], rest[NB:]
     halves, rest = rest[:NB], rest[NB:]
     early, rest = rest[:NB], rest[NB:]
     late, rest = rest[:NB], rest[NB:]
     pieces, rest = rest[:NB], rest[NB:]
-    (stat_send, stat_recv, in_send, in_recv, rs_send, rs_recv, fin_send, fin_own, fin_recv) = rest
+    (stat_send, stat_recv, in_send, in_recv, rs_send, rs_recv, fin_send, fin_own, mid_recv, mid_send, fin_recv) = rest
     genes, cells = own.shape[0] * own.shape[1], own.shape[2]
     S = genes // R
     nj = cells // 128
@@ -291,35 +291,58 @@
         for pair, t0, n, i, j, along in ROUNDS[r][1]:
             a, b, both = PAIRS[pair]
             ga, gb = gene_at(y, z, OFFSET[a]), gene_at(y, z, OFFSET[b])
-            if along == "j":
-                dst = final.at[i, j : j + n, pos]
-            else:
-                dst = final.at[i : i + n, j, pos]
-            yield pieces[r].at[t0 : t0 + n], dst, ga, gb, a == OWN
+            ti, tj = (i, slice(j, j + n)) if along == "j" else (slice(i, i + n), j)
+            yield pieces[r].at[t0 : t0 + n], ti, tj, ga, gb, a == OWN
             if both == "all":
-                yield pieces[r].at[t0 : t0 + n], dst, gb, ga, False
+                yield pieces[r].at[t0 : t0 + n], ti, tj, gb, ga, False
             if both == "below" and i:
-                yield pieces[r].at[t0 : t0 + i], final.at[0:i, i, pos], gb, ga, False
+                yield pieces[r].at[t0 : t0 + i], slice(0, i), i, gb, ga, False
+
+    def first_leg(r, src, ti, tj, row, col, sem):
+        to = {"cell": (col // 8) * 8 + c % 8, "gene": row}
+        return remote(src, mid.at[col % 8, ti, tj, zl], sem, mid_recv.at[col % 8], to)
 
     def s4(r):
         s = S // 16
         zl_copy(r).wait_recv()
         pieces[r][...] = pieces[r][...] + prods[r][:, 4 * core + x, pl.ds(zl * s, s)]
         k = 0
-        for src, dst, row, col, maybe in final_sends(r):
+        for src, ti, tj, row, col, maybe in final_sends(r):
             if maybe:
 
-                @pl.when(col == c)
+                @pl.when(col // 8 == zl)
                 def _():
-                    pltpu.make_async_copy(src, dst, fin_recv).start()
-
-                @pl.when(col != c)
+                    pltpu.make_async_copy(src, mid.at[col % 8, ti, tj, zl], mid_recv.at[col % 8]).start()
+
+                @pl.when(col // 8 != zl)
                 def _():
-                    remote(src, dst, fin_own.at[r, k], fin_recv, {"cell": col, "gene": row}).start()
+                    first_leg(r, src, ti, tj, row, col, fin_own.at[r, k]).start()
 
                 k += 1
             else:
-                remote(src, dst, fin_send, fin_recv, {"cell": col, "gene": row}).start()
+                first_leg(r, src, ti, tj, row, col, fin_send).start()
+
+    def second_leg(s):
+        dst = final.at[:, :, pl.ds(pos - zl, 2)]
+        return remote(mid.at[s], dst, mid_send.at[s], fin_recv, {"cell": zl * 8 + s})
+
+    def pass_final():
+        for d in range(8):
+            s = (c % 8 + d) % 8
+
+            @pl.when(zl * 8 + s == g)
+            def _():
+                lower = halves[0].at[:, 0:1]
+                pltpu.make_async_copy(lower, lower, mid_recv.at[s]).wait()
+
+            @pl.when(zl * 8 + s != g)
+            def _():
+                pltpu.make_async_copy(mid.at[s], mid.at[s], mid_recv.at[s]).wait()
+
+            if d:
+                second_leg(s).start()
+            else:
+                pltpu.make_async_copy(mid.at[s], final.at[:, :, pl.ds(pos - zl, 2)], fin_recv).start()
 
     compute_diagonal()
     s0(0)
@@ -354,7 +377,9 @@
     s4(NB - 2)
     s3(NB - 1)
     s4(NB - 1)
-
+    pass_final()
+
+    pltpu.make_async_copy(final, final, fin_recv).wait()
     dy, dz = (c // 4 - y + 4) % 4, (c % 4 - z + 4) % 4
 
     def among(offsets):
@@ -375,8 +400,6 @@
 
     @pl.when(diagonal)
     def _():
-        lower = prods[0].at[0 : len(below + even)]
-        pltpu.make_async_copy(lower, lower, fin_recv).wait()
         for i, j in below:
             write(i, j, tile(i, j))
             write(j, i, tile(i, j).T)
@@ -385,7 +408,6 @@
 
     @pl.when(jnp.logical_not(diagonal))
     def _():
-        pltpu.make_async_copy(final, final, fin_recv).wait()
 
         @pl.when(flip)
         def _():
@@ -420,16 +442,18 @@
             x_copy(r, k).wait_send()
         zl_copy(r).wait_send()
         k = 0
-        for src, dst, row, col, maybe in final_sends(r):
+        for src, ti, tj, row, col, maybe in final_sends(r):
             if maybe:
 
-                @pl.when(col != c)
+                @pl.when(col // 8 != zl)
                 def _():
-                    remote(src, dst, fin_own.at[r, k], fin_recv, {"cell": col, "gene": row}).wait_send()
+                    first_leg(r, src, ti, tj, row, col, fin_own.at[r, k]).wait_send()
 
                 k += 1
             else:
                 sent += src.shape[0]
+    for d in range(1, 8):
+        second_leg((c % 8 + d) % 8).wait_send()
     assert sent % 16 == 0
     pltpu.make_async_copy(prods[2].at[0 : sent // 16], prods[2].at[0 : sent // 16], fin_send).wait()
 
@@ -448,6 +472,7 @@
         pltpu.VMEM((NC, 8, 128), f32),
         pltpu.VMEM((R, S, cells), jnp.bfloat16),
         pltpu.VMEM((R, 5, S, cells), jnp.bfloat16),
+        pltpu.VMEM((8, R, R, 2, S // 16, S), f32),
         pltpu.VMEM((R, R, 16, S // 16, S), f32),
         *[pltpu.VMEM((n, 8, S // 8, S), f32) for n in ns],
         *[pltpu.VMEM((n, 4, S // 8, S), f32) for n in ns],
@@ -462,6 +487,8 @@
         dma((NB, 8)),
         dma(()),
         dma((NB, own_groups)),
+        dma((8,)),
+        dma((8,)),
         dma(()),
     ]
     return pl.pallas_call(

time: 159 us -> 147 us (0.925)
  Pallas kernels: 155 us -> 143 us
    pallas_call x1, Pallas kernels: 155 us -> 143 us  [body(): pl.pallas_call(kernel, out_shape=jax.ShapeDtypeStruct((genes, genes), f32...]
where the time goes in v5:
time: 147 us; the launch traced here: 145 us
  Pallas kernels  143 us (97%)
  local copies, waits for them, and re-layouts  2.26 us (2%)
    pallas_call x1, Pallas kernels, body(): pl.pallas_call(kernel, out_shape=jax.ShapeDtypeStruct((genes, genes), f32...  143 us

profile of v5, /device:TPU:33, one launch (start us, length us, event | category | flops | bytes accessed | tf_op | source)
XLA Modules:
  0.0 145.0 jit_solution(11729681580507415660)
XLA Ops:
  0.0 142.7 %shard_map.17 = f32[512,512]{1,0:T(8,128)} custom-call(s32[1024,512]{1,0:T(8,128)} %counts.1), custom_call_target="tpu_custom_call" | custom-call | tf_op jit(solution)/shard_map/pallas_call | solution.py:494
  142.7 2.3 %copy.3 = f32[512,512]{1,0:T(8,128)} copy(f32[512,512]{1,0:T(8,128)} %shard_map.17) | data formatting | bytes 2097152

commit v6 on v5

--- a/solution.py
+++ b/solution.py
@@ -18,7 +18,7 @@
     (OWN, OWN, None),
     (OWN, YP, "all"),
     (OWN, ZP, "all"),
-    (OWN, T, "all"),
+    (YP, ZM, "all"),
     (OWN, Y2, "all"),
     (YP, ZP, "all"),
     (ZM, Y2, "below"),
@@ -30,8 +30,17 @@
 MIRRORED = ((3, 0), (0, 3), (1, 1), (2, 1), (1, 3), (1, 2))
 
 
-EARLY_OWN, EARLY_BOTH = (1, 2), (5, 9)
-LATE_OWN, LATE_BOTH = (3, 4), (6, 7, 8)
+def whole_at(step):
+    found = []
+    if step < 2:
+        found += [(1, r) for r in range(2 * step, 2 * step + 2)]
+    if step < R:
+        found += [(2, step)]
+    if 0 < step < R:
+        found += [(pair, r) for r in range(0 if step == 1 else step, step + 1) for pair in (3, 5)]
+    if step:
+        found += [(4, step - 1)]
+    return found
 
 
 def plan():
@@ -47,14 +56,16 @@
         if step < 0:
             for i in range(R):
                 add(0, i + 1, i, 0, "j")
-        for r, alone, both in ((step, EARLY_OWN, EARLY_BOTH), (step - 1, LATE_OWN, LATE_BOTH)):
-            if 0 <= r < R:
-                for pair in alone:
-                    add(pair, R, 0, r, "i")
-                for pair in both:
-                    add(pair, r + 1, r, 0, "j")
-                    if r and PAIRS[pair][2] == "all":
-                        add(pair, r, 0, r, "i")
+        if step >= 0:
+            for pair, r in whole_at(step):
+                add(pair, R, 0, r, "i")
+            if step < R:
+                add(9, step + 1, step, 0, "j")
+            if step:
+                for pair in (6, 7, 8):
+                    add(pair, step, step - 1, 0, "j")
+                if step > 1:
+                    add(7, step - 1, 0, step - 1, "i")
         batches.append((n, groups))
     return batches
 
@@ -137,14 +148,6 @@
     grand = jnp.sum(jnp.sum(totbuf[...], axis=0)[0:1, :])
     share = depths / grand
     ceiling = float(NC * cells) ** 0.5
-    for q in range(nq):
-        r, o = (q * 128) // S, (q * 128) % S
-        for j in range(nj):
-            v = vt[j, q * 128 : (q + 1) * 128, :]
-            e = gcol[q] * share[j : j + 1, :]
-            s = (v - e) * lax.rsqrt(e + e * e / 100.0)
-            own[r, o : o + 128, j * 128 : (j + 1) * 128] = jnp.clip(s, -ceiling, ceiling).astype(jnp.bfloat16)
-
     def part(h):
         return slice(h * (S // H), (h + 1) * (S // H))
 
@@ -164,11 +167,17 @@
         for h in range(H):
             arrived(b, r, h)
 
+    assert S == 128
     for r in range(R):
+        for j in range(nj):
+            v = vt[j, r * S : (r + 1) * S, :]
+            e = gcol[r] * share[j : j + 1, :]
+            t = (v - e) * lax.rsqrt(e + e * e / 100.0)
+            own[r, :, j * 128 : (j + 1) * 128] = jnp.clip(t, -ceiling, ceiling).astype(jnp.bfloat16)
         for h in range(H):
             own_to(ZM, r, h, to_zp).start()
             own_to(ZP, r, h, to_zm).start()
-        if r < 1:
+        if r < 2:
             for h in range(H):
                 own_to(YP, r, h, to_ym).start()
 
@@ -190,34 +199,27 @@
             for j in range(i + 1):
                 put(0, i * (i + 1) // 2 + j, d[:, j * S : (j + 1) * S])
 
+    def whole(m, pairs):
+        for pair, t0, n, _, j, along in ROUNDS[m][1]:
+            if pair in pairs:
+                a, b, _ = PAIRS[pair]
+
+                @pl.loop(0, R)
+                def _(i):
+                    left = own[i] if a == OWN else got[i, a]
+                    put(m, t0 + i, nt(left, got[j, b]))
+
     def compute_early(m):
         base, e = base_of(m), m - 1
-
-        @pl.loop(0, R)
-        def _(i):
-            d = nt(own[i], got[e, YP : ZP + 1].reshape(2 * S, cells))
-            for k in range(2):
-                put(m, base[k + 1, "i"] + i, d[:, k * S : (k + 1) * S])
+        whole(m, (1, 2, 3, 5))
 
         @pl.loop(0, e + 1)
         def _(j):
-            put(m, base[5, "j"] + j, nt(got[e, YP], got[j, ZP]))
             put(m, base[9, "j"] + j, nt(got[e, ZP], got[j, ZM]))
-
-        if e:
-
-            @pl.loop(0, e)
-            def _(i):
-                put(m, base[5, "i"] + i, nt(got[i, YP], got[e, ZP]))
 
     def compute_late(m):
         base, l = base_of(m), m - 2
-
-        @pl.loop(0, R)
-        def _(i):
-            d = nt(own[i], got[l, T : Y2 + 1].reshape(2 * S, cells))
-            for k in range(2):
-                put(m, base[k + 3, "i"] + i, d[:, k * S : (k + 1) * S])
+        whole(m, (4,))
 
         @pl.loop(0, l + 1)
         def _(j):
@@ -300,7 +302,7 @@
 
     def first_leg(r, src, ti, tj, row, col, sem):
         to = {"cell": (col // 8) * 8 + c % 8, "gene": row}
-        return remote(src, mid.at[col % 8, ti, tj, zl], sem, mid_recv.at[col % 8], to)
+        return remote(src, mid.at[col % 8, ti, tj, zl], sem, mid_recv.at[r // (NB - 1), col % 8], to)
 
     def s4(r):
         s = S // 16
@@ -312,7 +314,7 @@
 
                 @pl.when(col // 8 == zl)
                 def _():
-                    pltpu.make_async_copy(src, mid.at[col % 8, ti, tj, zl], mid_recv.at[col % 8]).start()
+                    pltpu.make_async_copy(src, mid.at[col % 8, ti, tj, zl], mid_recv.at[r // (NB - 1), col % 8]).start()
 
                 @pl.when(col // 8 != zl)
                 def _():
@@ -322,27 +324,51 @@
             else:
                 first_leg(r, src, ti, tj, row, col, fin_send).start()
 
-    def second_leg(s):
-        dst = final.at[:, :, pl.ds(pos - zl, 2)]
-        return remote(mid.at[s], dst, mid_send.at[s], fin_recv, {"cell": zl * 8 + s})
-
-    def pass_final():
+    regions = ((slice(0, R - 1), slice(0, R - 1)), (R - 1, slice(0, R)), (slice(0, R - 1), R - 1))
+
+    def second_leg(s, k):
+        ti, tj = regions[k]
+        dst = final.at[ti, tj, pl.ds(pos - zl, 2)]
+        return remote(mid.at[s, ti, tj], dst, mid_send.at[k, s], fin_recv, {"cell": zl * 8 + s})
+
+    def pass_final(phase):
+        inner, rows = (R - 1) * (R - 1), R * (R - 1)
         for d in range(8):
             s = (c % 8 + d) % 8
-
-            @pl.when(zl * 8 + s == g)
+            col = zl * 8 + s
+            dy, dz = (col // 4 - y + 4) % 4, (col % 4 - z + 4) % 4
+            diagonal = col == g
+            lagging = (dy == 2) & ((dz == 1) | (dz == 3))
+            inward = ((dz == 2) & (dy != 0)) | ((dz == 0) & (dy == 2))
+
+            def await_tiles(n):
+                like = late[2].at[0, 0:n]
+                pltpu.make_async_copy(like, like, mid_recv.at[phase, s]).wait()
+
+            @pl.when(lagging)
             def _():
-                lower = halves[0].at[:, 0:1]
-                pltpu.make_async_copy(lower, lower, mid_recv.at[s]).wait()
-
-            @pl.when(zl * 8 + s != g)
+                await_tiles(R if phase else rows)
+
+            @pl.when(inward)
             def _():
-                pltpu.make_async_copy(mid.at[s], mid.at[s], mid_recv.at[s]).wait()
-
-            if d:
-                second_leg(s).start()
-            else:
-                pltpu.make_async_copy(mid.at[s], final.at[:, :, pl.ds(pos - zl, 2)], fin_recv).start()
+                await_tiles(R * R - inner if phase else inner)
+
+            if phase == 0:
+
+                @pl.when(diagonal)
+                def _():
+                    await_tiles(R * (R + 1) // 2)
+
+                @pl.when(jnp.logical_not(diagonal | lagging | inward))
+                def _():
+                    await_tiles(R * R)
+
+            for k in (1, 2) if phase else (0,):
+                if d:
+                    second_leg(s, k).start()
+                else:
+                    ti, tj = regions[k]
+                    pltpu.make_async_copy(mid.at[s, ti, tj], final.at[ti, tj, pl.ds(pos - zl, 2)], fin_recv).start()
 
     compute_diagonal()
     s0(0)
@@ -354,12 +380,14 @@
         if k < R:
             for h in range(1, H):
                 pass_on(k, h)
-            if k + 1 < R:
-                for h in range(H):
-                    own_to(YP, k + 1, h, to_ym).start()
+            if k == 0:
+                for r in range(2, R):
+                    for h in range(H):
+                        own_to(YP, r, h, to_ym).start()
         if k < R:
             have(ZP, k)
-            have(YP, k)
+            for r in range(2 * k, 2 * k + 2 if k < 2 else 0):
+                have(YP, r)
             compute_early(m)
         if k:
             have(T, k - 1)
@@ -377,7 +405,8 @@
     s4(NB - 2)
     s3(NB - 1)
     s4(NB - 1)
-    pass_final()
+    pass_final(0)
+    pass_final(1)
 
     pltpu.make_async_copy(final, final, fin_recv).wait()
     dy, dz = (c // 4 - y + 4) % 4, (c % 4 - z + 4) % 4
@@ -453,7 +482,8 @@
             else:
                 sent += src.shape[0]
     for d in range(1, 8):
-        second_leg((c % 8 + d) % 8).wait_send()
+        for k in range(3):
+            second_leg((c % 8 + d) % 8, k).wait_send()
     assert sent % 16 == 0
     pltpu.make_async_copy(prods[2].at[0 : sent // 16], prods[2].at[0 : sent // 16], fin_send).wait()
 
@@ -487,8 +517,8 @@
         dma((NB, 8)),
         dma(()),
         dma((NB, own_groups)),
-        dma((8,)),
-        dma((8,)),
+        dma((2, 8)),
+        dma((3, 8)),
         dma(()),
     ]
     return pl.pallas_call(

time: 147 us -> 152 us (1.034)
  the two profiles are of different devices: /device:TPU:33 before, /device:TPU:1 now
where the time goes in v6:
time: 152 us
  Pallas kernels  150 us (99%)
  local copies, waits for them, and re-layouts  2.26 us (1%)
    pallas_call x1, Pallas kernels, body(): pl.pallas_call(kernel, out_shape=jax.ShapeDtypeStruct((genes, genes), f32...  150 us

profile of v6, /device:TPU:1, one launch (start us, length us, event | category | flops | bytes accessed | tf_op | source)
XLA Modules:
  0.0 152.2 jit_solution(7169782598281802391)
XLA Ops:
  0.0 150.0 %shard_map.17 = f32[512,512]{1,0:T(8,128)} custom-call(s32[1024,512]{1,0:T(8,128)} %counts.1), custom_call_target="tpu_custom_call" | custom-call | tf_op jit(solution)/shard_map/pallas_call | solution.py:524
  150.0 2.3 %copy.3 = f32[512,512]{1,0:T(8,128)} copy(f32[512,512]{1,0:T(8,128)} %shard_map.17) | data formatting | bytes 2097152

commit v7 on v6

--- a/solution.py
+++ b/solution.py
@@ -200,39 +200,39 @@
                 put(0, i * (i + 1) // 2 + j, d[:, j * S : (j + 1) * S])
 
     def whole(m, pairs):
-        for pair, t0, n, _, j, along in ROUNDS[m][1]:
-            if pair in pairs:
-                a, b, _ = PAIRS[pair]
-
-                @pl.loop(0, R)
+        for a in (OWN, YP):
+            cols = [(gr[1], gr[4], PAIRS[gr[0]][1]) for gr in ROUNDS[m][1] if gr[0] in pairs and PAIRS[gr[0]][0] == a]
+            for two in (cols[k : k + 2] for k in range(0, len(cols), 2)):
+
+                @pl.loop(0, R // 2)
                 def _(i):
-                    left = own[i] if a == OWN else got[i, a]
-                    put(m, t0 + i, nt(left, got[j, b]))
+                    rows = pl.ds(2 * i, 2)
+                    left = (own[rows] if a == OWN else got[rows, a]).reshape(2 * S, cells)
+                    right = [got[j, b] for _, j, b in two]
+                    d = nt(left, jnp.concatenate(right, axis=0) if len(two) > 1 else right[0])
+                    for u in range(2):
+                        for k, (t0, _, _) in enumerate(two):
+                            put(m, t0 + 2 * i + u, d[u * S : (u + 1) * S, k * S : (k + 1) * S])
+
+    def corner(m, pair, r):
+        (a, b, _), t0 = PAIRS[pair], base_of(m)[pair, "j"]
+        d = nt(got[r, a], got[0 : r + 1, b].reshape((r + 1) * S, cells))
+        for j in range(r + 1):
+            put(m, t0 + j, d[:, j * S : (j + 1) * S])
 
     def compute_early(m):
-        base, e = base_of(m), m - 1
         whole(m, (1, 2, 3, 5))
-
-        @pl.loop(0, e + 1)
-        def _(j):
-            put(m, base[9, "j"] + j, nt(got[e, ZP], got[j, ZM]))
+        corner(m, 9, m - 1)
 
     def compute_late(m):
         base, l = base_of(m), m - 2
         whole(m, (4,))
-
-        @pl.loop(0, l + 1)
-        def _(j):
-            d = nt(got[l, ZP], got[j, T : Y2 + 1].reshape(2 * S, cells))
-            for k in range(2):
-                put(m, base[k + 7, "j"] + j, d[:, k * S : (k + 1) * S])
-            put(m, base[6, "j"] + j, nt(got[l, ZM], got[j, Y2]))
-
+        for pair in (6, 7, 8):
+            corner(m, pair, l)
         if l:
-
-            @pl.loop(0, l)
-            def _(i):
-                put(m, base[7, "i"] + i, nt(got[i, ZP], got[l, T]))
+            d = nt(got[0:l, ZP].reshape(l * S, cells), got[l, T])
+            for i in range(l):
+                put(m, base[7, "i"] + i, d[i * S : (i + 1) * S])
 
     def rs(r, k, src, dst, device):
         return remote(src, dst, rs_send.at[r, k], rs_recv.at[r, k], device)
@@ -373,7 +373,6 @@
     compute_diagonal()
     s0(0)
     s1(0)
-    s2(0)
     pass_on(0, 0)
     for k in range(R + 1):
         m = k + 1
@@ -394,14 +393,23 @@
             have(Y2, k - 1)
             compute_late(m)
         s0(m)
+        if k == R:
+            s1(m)
+            s3(m - 1)
+            s2(m)
+            continue
+        s2(m - 1)
+        if k:
+            s3(m - 2)
         s1(m)
         if k + 1 < R:
             pass_on(k + 1, 0)
+            continue
+        for done in range(m - 1):
+            s4(done)
+        s2(m)
         s3(m - 1)
-        s2(m)
-        if k == R - 1:
-            for done in range(m):
-                s4(done)
+        s4(m - 1)
     s4(NB - 2)
     s3(NB - 1)
     s4(NB - 1)

time: 152 us -> 138 us (0.908)
  the two profiles are of different devices: /device:TPU:1 before, /device:TPU:33 now
where the time goes in v7:
time: 138 us
  Pallas kernels  136 us (99%)
  local copies, waits for them, and re-layouts  2.26 us (2%)
    pallas_call x1, Pallas kernels, body(): pl.pallas_call(kernel, out_shape=jax.ShapeDtypeStruct((genes, genes), f32...  136 us

profile of v7, /device:TPU:33, one launch (start us, length us, event | category | flops | bytes accessed | tf_op | source)
XLA Modules:
  0.0 138.2 jit_solution(5686028014960464813)
XLA Ops:
  0.0 136.0 %shard_map.17 = f32[512,512]{1,0:T(8,128)} custom-call(s32[1024,512]{1,0:T(8,128)} %counts.1), custom_call_target="tpu_custom_call" | custom-call | tf_op jit(solution)/shard_map/pallas_call | solution.py:532
  136.0 2.3 %copy.3 = f32[512,512]{1,0:T(8,128)} copy(f32[512,512]{1,0:T(8,128)} %shard_map.17) | data formatting | bytes 2097152

commit v8 on v7

--- a/solution.py
+++ b/solution.py
@@ -9,7 +9,7 @@
 
 MESH = pl.DeviceIdType.MESH
 R = 4
-H = 2
+H = 4
 NC = 16
 YP, ZP, T, Y2, ZM = range(5)
 OWN = -1
@@ -329,7 +329,7 @@
     def second_leg(s, k):
         ti, tj = regions[k]
         dst = final.at[ti, tj, pl.ds(pos - zl, 2)]
-        return remote(mid.at[s, ti, tj], dst, mid_send.at[k, s], fin_recv, {"cell": zl * 8 + s})
+        return remote(mid.at[s, ti, tj], dst, mid_send.at[k, s], fin_recv.at[min(k, 1)], {"cell": zl * 8 + s})
 
     def pass_final(phase):
         inner, rows = (R - 1) * (R - 1), R * (R - 1)
@@ -368,16 +368,17 @@
                     second_leg(s, k).start()
                 else:
                     ti, tj = regions[k]
-                    pltpu.make_async_copy(mid.at[s, ti, tj], final.at[ti, tj, pl.ds(pos - zl, 2)], fin_recv).start()
+                    pltpu.make_async_copy(mid.at[s, ti, tj], final.at[ti, tj, pl.ds(pos - zl, 2)], fin_recv.at[min(k, 1)]).start()
 
     compute_diagonal()
     s0(0)
     s1(0)
-    pass_on(0, 0)
+    for h in range(H // 2):
+        pass_on(0, h)
     for k in range(R + 1):
         m = k + 1
         if k < R:
-            for h in range(1, H):
+            for h in range(H // 2, H):
                 pass_on(k, h)
             if k == 0:
                 for r in range(2, R):
@@ -403,7 +404,8 @@
             s3(m - 2)
         s1(m)
         if k + 1 < R:
-            pass_on(k + 1, 0)
+            for h in range(H // 2):
+                pass_on(k + 1, h)
             continue
         for done in range(m - 1):
             s4(done)
@@ -416,7 +418,6 @@
     pass_final(0)
     pass_final(1)
 
-    pltpu.make_async_copy(final, final, fin_recv).wait()
     dy, dz = (c // 4 - y + 4) % 4, (c % 4 - z + 4) % 4
 
     def among(offsets):
@@ -431,40 +432,39 @@
     def tile(i, j):
         return final[i, j].reshape(S, S) * scale
 
-    below = [(i, j) for i in range(R) for j in range(i)]
-    above = [(i, j) for j, i in below]
-    even = [(i, i) for i in range(R)]
-
-    @pl.when(diagonal)
-    def _():
-        for i, j in below:
-            write(i, j, tile(i, j))
-            write(j, i, tile(i, j).T)
-        for i, j in even:
-            write(i, j, tile(i, j))
-
-    @pl.when(jnp.logical_not(diagonal))
-    def _():
+    first = R - 1
+    for tiles in ([(i, j) for i in range(first) for j in range(first)], [(i, j) for i in range(R) for j in range(R) if first in (i, j)]):
+        phase = int(len(tiles) < first * first)
+        like = prods[2].at[0 : len(tiles)]
+        pltpu.make_async_copy(like, like, fin_recv.at[phase]).wait()
+        lower = [t for t in tiles if t[0] >= t[1]]
+        above = [t for t in tiles if t[0] < t[1]]
 
         @pl.when(flip)
         def _():
-            for i, j in below + even + above:
+            for i, j in tiles:
                 write(j, i, tile(i, j).T)
 
         @pl.when(jnp.logical_not(flip))
         def _():
-            for i, j in below + even:
+            for i, j in lower:
                 write(i, j, tile(i, j))
 
-            @pl.when(halved)
-            def _():
-                for i, j in above:
-                    write(i, j, tile(i, j).T)
-
-            @pl.when(jnp.logical_not(halved))
-            def _():
-                for i, j in above:
-                    write(i, j, tile(i, j))
+        @pl.when(diagonal)
+        def _():
+            for i, j in lower:
+                if i > j:
+                    write(j, i, tile(i, j).T)
+
+        @pl.when(halved)
+        def _():
+            for i, j in above:
+                write(i, j, tile(i, j).T)
+
+        @pl.when(jnp.logical_not(flip | diagonal | halved))
+        def _():
+            for i, j in above:
+                write(i, j, tile(i, j))
 
     for k, buf in ((0, colbuf), (1, rowbuf), (2, totbuf)):
         others(buf, stat_send.at[k]).wait()
@@ -527,7 +527,7 @@
         dma((NB, own_groups)),
         dma((2, 8)),
         dma((3, 8)),
-        dma(()),
+        dma((2,)),
     ]
     return pl.pallas_call(
         kernel,

time: 138 us -> 140 us (1.014); the launches traced: 138 us -> 137 us
  no operation moved by 1% of the time
where the time goes in v8:
time: 140 us; the launch traced here: 137 us
  Pallas kernels  135 us (96%)
  local copies, waits for them, and re-layouts  2.26 us (2%)
    pallas_call x1, Pallas kernels, body(): pl.pallas_call(kernel, out_shape=jax.ShapeDtypeStruct((genes, genes), f32...  135 us

profile of v8, /device:TPU:33, one launch (start us, length us, event | category | flops | bytes accessed | tf_op | source)
XLA Modules:
  0.0 137.3 jit_solution(9023457068280601573)
XLA Ops:
  0.0 135.1 %shard_map.17 = f32[512,512]{1,0:T(8,128)} custom-call(s32[1024,512]{1,0:T(8,128)} %counts.1), custom_call_target="tpu_custom_call" | custom-call | tf_op jit(solution)/shard_map/pallas_call | solution.py:532
  135.1 2.3 %copy.3 = f32[512,512]{1,0:T(8,128)} copy(f32[512,512]{1,0:T(8,128)} %shard_map.17) | data formatting | bytes 2097152

commit v9 on v8

--- a/solution.py
+++ b/solution.py
@@ -9,7 +9,7 @@
 
 MESH = pl.DeviceIdType.MESH
 R = 4
-H = 4
+H = 2
 NC = 16
 YP, ZP, T, Y2, ZM = range(5)
 OWN = -1
@@ -395,8 +395,9 @@
             compute_late(m)
         s0(m)
         if k == R:
+            s3(m - 1)
             s1(m)
-            s3(m - 1)
+            s4(m - 1)
             s2(m)
             continue
         s2(m - 1)
@@ -407,12 +408,12 @@
             for h in range(H // 2):
                 pass_on(k + 1, h)
             continue
-        for done in range(m - 1):
+        s4(0)
+        s2(m)
+        for done in range(1, m - 1):
             s4(done)
-        s2(m)
         s3(m - 1)
         s4(m - 1)
-    s4(NB - 2)
     s3(NB - 1)
     s4(NB - 1)
     pass_final(0)

time: 140 us -> 139 us (level); the launches traced: 137 us -> 139 us
  Pallas kernels: 135 us -> 137 us
    pallas_call x1, Pallas kernels: 135 us -> 137 us  [body(): pl.pallas_call(kernel, out_shape=jax.ShapeDtypeStruct((genes, genes), f32...]
where the time goes in v9:
time: 139 us
  Pallas kernels  137 us (99%)
  local copies, waits for them, and re-layouts  2.26 us (2%)
    pallas_call x1, Pallas kernels, body(): pl.pallas_call(kernel, out_shape=jax.ShapeDtypeStruct((genes, genes), f32...  137 us

profile of v9, /device:TPU:33, one launch (start us, length us, event | category | flops | bytes accessed | tf_op | source)
XLA Modules:
  0.0 139.0 jit_solution(15825861848141032934)
XLA Ops:
  0.0 136.7 %shard_map.17 = f32[512,512]{1,0:T(8,128)} custom-call(s32[1024,512]{1,0:T(8,128)} %counts.1), custom_call_target="tpu_custom_call" | custom-call | tf_op jit(solution)/shard_map/pallas_call | solution.py:533
  136.7 2.3 %copy.3 = f32[512,512]{1,0:T(8,128)} copy(f32[512,512]{1,0:T(8,128)} %shard_map.17) | data formatting | bytes 2097152

commit v10 on v7

--- a/solution.py
+++ b/solution.py
@@ -160,8 +160,12 @@
     def pass_on(k, h):
         arrived(ZM, k, h)
         src = got.at[k, ZM, part(h)]
-        for b, device in ((T, to_yp), (Y2, to_y2)):
+        for b, device in ((T, to_yp), (Y2, to_y2)) if h else ((T, to_yp),):
             remote(src, got.at[k, b, part(h)], in_send.at[b, k, h], in_recv.at[b, k, h], device).start()
+        if h == H - 1:
+            arrived(T, k, 0)
+            src = got.at[k, T, part(0)]
+            remote(src, got.at[k, Y2, part(0)], in_send.at[Y2, k, 0], in_recv.at[Y2, k, 0], to_yp).start()
 
     def have(b, r):
         for h in range(H):
@@ -389,7 +393,8 @@
                 have(YP, r)
             compute_early(m)
         if k:
-            have(T, k - 1)
+            for h in range(1, H):
+                arrived(T, k - 1, h)
             have(Y2, k - 1)
             compute_late(m)
         s0(m)

time: 138 us -> 141 us (1.022); the launches traced: 138 us -> 139 us
  no operation moved by 1% of the time
where the time goes in v10:
time: 141 us; the launch traced here: 139 us
  Pallas kernels  137 us (97%)
  local copies, waits for them, and re-layouts  2.26 us (2%)
    pallas_call x1, Pallas kernels, body(): pl.pallas_call(kernel, out_shape=jax.ShapeDtypeStruct((genes, genes), f32...  137 us

profile of v10, /device:TPU:33, one launch (start us, length us, event | category | flops | bytes accessed | tf_op | source)
XLA Modules:
  0.0 138.8 jit_solution(12190581014544903730)
XLA Ops:
  0.0 136.5 %shard_map.17 = f32[512,512]{1,0:T(8,128)} custom-call(s32[1024,512]{1,0:T(8,128)} %counts.1), custom_call_target="tpu_custom_call" | custom-call | tf_op jit(solution)/shard_map/pallas_call | solution.py:537
  136.5 2.3 %copy.3 = f32[512,512]{1,0:T(8,128)} copy(f32[512,512]{1,0:T(8,128)} %shard_map.17) | data formatting | bytes 2097152

commit v11 on v7

--- a/solution.py
+++ b/solution.py
@@ -78,7 +78,8 @@
     return ((y + offset[0]) % 4) * 4 + (z + offset[1]) % 4
 
 
-def kernel(counts, out, *scratch):
+def kernel(counts_hbm, out, *scratch):
+    (counts, counts_sem), scratch = scratch[:2], scratch[2:]
     (vt, colbuf, rowbuf, totbuf, own, got, mid, final), rest = scratch[:8], scratch[8:]
     prods, rest = rest[:NB], rest[NB:]
     halves, rest = rest[:NB], rest[NB:]
@@ -109,11 +110,14 @@
             src_ref=src, dst_ref=dst, send_sem=ssem, recv_sem=rsem, device_id=device, device_id_type=MESH
         )
 
+    load = pltpu.make_async_copy(counts_hbm, counts, counts_sem)
+    load.start()
     barrier = pltpu.get_barrier_semaphore()
     for k in range(1, NC):
         pl.semaphore_signal(barrier, inc=1, device_id={"cell": (c + k) % NC}, device_id_type=MESH)
         pl.semaphore_signal(barrier, inc=1, device_id={"gene": (g + k) % NC}, device_id_type=MESH)
 
+    load.wait()
     def local(j, acc):
         v = counts[pl.ds(j * 128, 128), :].astype(jnp.float32)
         t = v.T
@@ -423,13 +427,12 @@
         return functools.reduce(jnp.logical_or, [(dy == a) & (dz == b) for a, b in offsets])
 
     diagonal, halved, flip = among(((0, 0),)), among(HALVED), among(MIRRORED)
-    scale = 1.0 / float(NC * cells)
 
     def write(i, j, tile):
         out[i * S : (i + 1) * S, j * S : (j + 1) * S] = tile
 
     def tile(i, j):
-        return final[i, j].reshape(S, S) * scale
+        return final[i, j].reshape(S, S)
 
     below = [(i, j) for i in range(R) for j in range(i)]
     above = [(i, j) for j, i in below]
@@ -504,6 +507,8 @@
     dma = pltpu.SemaphoreType.DMA
     own_groups = max(sum(PAIRS[gr[0]][0] == OWN for gr in groups) for _, groups in ROUNDS)
     scratch = [
+        pltpu.VMEM((cells, genes), jnp.int32),
+        dma(()),
         pltpu.VMEM((cells // 128, genes, 128), f32),
         pltpu.VMEM((NC, 8, 128), f32),
         pltpu.VMEM((NC, 8, 128), f32),
@@ -529,16 +534,17 @@
         dma((3, 8)),
         dma(()),
     ]
-    return pl.pallas_call(
+    total = pl.pallas_call(
         kernel,
         out_shape=jax.ShapeDtypeStruct((genes, genes), f32),
-        in_specs=[pl.BlockSpec(memory_space=pltpu.VMEM)],
+        in_specs=[pl.BlockSpec(memory_space=pl.ANY)],
         out_specs=pl.BlockSpec(memory_space=pltpu.VMEM),
         scratch_shapes=scratch,
         compiler_params=pltpu.CompilerParams(
             collective_id=0, has_side_effects=True, vmem_limit_bytes=60 * 1024 * 1024
         ),
     )(counts)
+    return total / jnp.float32(NC * cells)
 
 
 def solution(mesh):

time: 138 us -> 136 us (0.986); the launches traced: 138 us -> 134 us
  Pallas kernels: 136 us -> 131 us
  other arithmetic: 0 us -> 2.29 us
  local copies, waits for them, and re-layouts: 2.26 us -> 0 us
    pallas_call x1, Pallas kernels: 136 us -> 131 us  [body(): pl.pallas_call(kernel, out_shape=jax.ShapeDtypeStruct((genes, genes), f32...]
    div x0 -> x1, other arithmetic: none -> 2.29 us  [body(): return total / jnp.float32(NC * cells)]
    unnamed x1 -> x0, local copies, waits for them, and re-layouts: 2.26 us -> none
where the time goes in v11:
time: 136 us; the launch traced here: 134 us
  Pallas kernels  131 us (96%)
  other arithmetic  2.29 us (2%)
    pallas_call x1, Pallas kernels, body(): pl.pallas_call(kernel, out_shape=jax.ShapeDtypeStruct((genes, genes), f32...  131 us

profile of v11, /device:TPU:33, one launch (start us, length us, event | category | flops | bytes accessed | tf_op | source)
XLA Modules:
  0.0 133.7 jit_solution(13654884852108182296)
XLA Ops:
  0.0 131.4 %shard_map.17 = f32[512,512]{1,0:T(8,128)} custom-call(s32[1024,512]{1,0:T(8,128)} %counts_hbm.1), custom_call_target="tpu_custom_call" | custom-call | tf_op jit(solution)/shard_map/pallas_call | solution.py:537
  131.4 2.3 %broadcast_multiply_fusion = f32[512,512]{1,0:T(8,128)} fusion(f32[512,512]{1,0:T(8,128)} %shard_map.17), kind=kLoop, calls=%fused_computation | loop fusion | flops 262144 | bytes 2097152 | tf_op jit(solution)/shard_map/div | solution.py:547

commit v12 on v11

--- a/solution.py
+++ b/solution.py
@@ -398,8 +398,9 @@
             compute_late(m)
         s0(m)
         if k == R:
+            s3(m - 1)
             s1(m)
-            s3(m - 1)
+            s4(m - 1)
             s2(m)
             continue
         s2(m - 1)
@@ -414,7 +415,6 @@
         s2(m)
         s3(m - 1)
         s4(m - 1)
-    s4(NB - 2)
     s3(NB - 1)
     s4(NB - 1)
     pass_final(0)

time: 136 us -> 134 us (0.985); the launches traced: 134 us -> 133 us
  no operation moved by 1% of the time
where the time goes in v12:
time: 134 us; the launch traced here: 133 us
  Pallas kernels  131 us (98%)
  other arithmetic  2.29 us (2%)
    pallas_call x1, Pallas kernels, body(): pl.pallas_call(kernel, out_shape=jax.ShapeDtypeStruct((genes, genes), f32...  131 us

profile of v12, /device:TPU:33, one launch (start us, length us, event | category | flops | bytes accessed | tf_op | source)
XLA Modules:
  0.0 133.2 jit_solution(4099477849223976017)
XLA Ops:
  0.0 130.9 %shard_map.17 = f32[512,512]{1,0:T(8,128)} custom-call(s32[1024,512]{1,0:T(8,128)} %counts_hbm.1), custom_call_target="tpu_custom_call" | custom-call | tf_op jit(solution)/shard_map/pallas_call | solution.py:537
  130.9 2.3 %broadcast_multiply_fusion = f32[512,512]{1,0:T(8,128)} fusion(f32[512,512]{1,0:T(8,128)} %shard_map.17), kind=kLoop, calls=%fused_computation | loop fusion | flops 262144 | bytes 2097152 | tf_op jit(solution)/shard_map/div | solution.py:547
